TPU v7x, 32 devices: a whole 2x2x4 slice. The times are simulated.
32 devices in a mesh: band: 4 (over y, core), grid: 8 (over z, x).
Axes of the slice: x: 2, y: 2, z: 4, core: 2. Of those that a mesh axis runs over, the one named last changes fastest.
Arguments:
- orbitals: float32 [64, 16, 4096], P('band', 'grid'), may hold values from -6 to 6
- potential: float32 [16, 4096], P('grid'), may hold values from 0 to 2
Outputs:
- rotated: bfloat16 [64, 16, 4096], P('band', 'grid')
All inputs are finite; a program needn't handle non-finite values. Where the computation divides by a largest or mean magnitude, that divisor is 1e-20 or more.
Results may differ from a plain program's by a relative error of at most 0.001.
The roundings to bfloat16 on the way count: a program that leaves them out, or rounds other values in their place, can miss the bound.
Values may be sent and summed in bfloat16 or wider, within the bound.
A program may use at most 64 MiB of HBM per device.

v0:
```python
import jax
import jax.numpy as jnp
from jax import lax
from jax.sharding import PartitionSpec as P

NX = 64
DEGREE = 2
NS_ITERS = 2


def with_halo(block, sides, width):
    for axis, dim in sides:
        count = lax.axis_size(axis)
        forward = [(i, i + 1) for i in range(count - 1)]
        forward.append((count - 1, 0))
        backward = [(target, source) for source, target in forward]
        low = lax.ppermute(
            lax.slice_in_dim(block, block.shape[dim] - width, None, axis=dim), axis, forward
        )
        high = lax.ppermute(lax.slice_in_dim(block, 0, width, axis=dim), axis, backward)
        block = jnp.concatenate([low, block, high], axis=dim)
    return block


def apply_inner(extended, potential):
    inner = extended[:, 1:-1]
    count = inner.shape[0]
    planes = inner.shape[1]
    square = inner.reshape(count, planes, NX, NX)
    sideways = jnp.roll(square, 1, 2) + jnp.roll(square, -1, 2)
    sideways = sideways + jnp.roll(square, 1, 3) + jnp.roll(square, -1, 3)
    beside = extended[:, 2:] + extended[:, :-2] + sideways.reshape(inner.shape)
    return 0.5 * (6.0 * inner - beside) + potential[None] * inner


def local(orbitals, potential):
    previous = orbitals
    current = orbitals
    for degree_step in range(DEGREE):
        extended = with_halo(current, (("grid", 1),), 1)
        applied = apply_inner(extended, potential)
        if degree_step == 0:
            following = (applied - 5.0 * current) / 3.0
        else:
            following = 2.0 * (applied - 5.0 * current) / 3.0 - previous
        previous = current
        current = following
    count, zplanes, width = orbitals.shape
    filtered = current.astype(jnp.bfloat16).reshape(count, zplanes * width)
    pieces = lax.all_to_all(filtered, "band", split_axis=1, concat_axis=0, tiled=True)
    total_cells = pieces.shape[1] * lax.axis_size("band") * lax.axis_size("grid")
    partial_value = (
        lax.dot_general(
            pieces, pieces, (((1,), (1,)), ((), ())), preferred_element_type=jnp.float32
        )
        / total_cells
    )
    gram = lax.psum(partial_value, ("band", "grid"))
    scale = jnp.max(jnp.sum(jnp.abs(gram), axis=1))
    identity_mat = jnp.eye(gram.shape[0], dtype=jnp.float32)
    upper = gram / scale
    lower = identity_mat
    for sweep in range(NS_ITERS):
        factor = 1.5 * identity_mat - 0.5 * jnp.dot(lower, upper, precision=lax.Precision.HIGHEST)
        upper = jnp.dot(upper, factor, precision=lax.Precision.HIGHEST)
        lower = jnp.dot(factor, lower, precision=lax.Precision.HIGHEST)
    root = (lower / jnp.sqrt(scale)).astype(jnp.bfloat16)
    turned = lax.dot_general(
        root, pieces, (((0,), (0,)), ((), ())), preferred_element_type=jnp.float32
    )
    turned = turned.astype(jnp.bfloat16)
    returned = lax.all_to_all(turned, "band", split_axis=0, concat_axis=1, tiled=True)
    return returned.reshape(count, zplanes, width)


def solution(mesh):
    placed = (P("band", "grid", None), P("grid", None))
    return jax.shard_map(
        local, mesh=mesh, in_specs=placed, out_specs=P("band", "grid", None), check_vma=False
    )
```

profile of v0, /device:TPU:0, one launch (start us, length us, event | category | flops | bytes accessed | tf_op | source)
XLA Modules:
  0.0 102.4 jit_solution(3121627851999156750)
XLA Ops:
  0.0 1.9 %fusion.24 = (f32[16,1,4096]{2,1,0:T(1,128)S(1)}, f32[16,1,4096]{2,1,0:T(1,128)S(1)}) fusion(f32[16,2,4096]{2,1,0:T(2,128)} %param.2), kind=kLoop, calls=%fused_computation.42 | loop fusion | bytes 1048576 | tf_op jit(solution)/shard_map/slice | solution.py:20
  1.9 6.1 %collective-permute-start = (f32[16,1,4096]{2,1,0:T(1,128)S(1)}, f32[16,1,4096]{2,1,0:T(1,128)S(1)}, u32[]{:S(2)}, u32[]{:S(2)}) collective-permute-start(f32[16,1,4096]{2,1,0:T(1,128)S(1)} %get-tuple-element.25), channel_id=1, source_target_pairs={{1,0},{2,1},{3,2},{4,3},{5,4},{6,5},{7,6},{0,7},{9,8},{10,9},{11,1... | collective-permute-start | bytes 786440 | tf_op jit(solution)/shard_map/ppermute | solution.py:20
  7.9 0.6 reshape.35
  8.6 0.4 fusion.19
  9.5 0.5 copy-done.1
  10.1 0.9 fusion.4
  11.0 0.5 add.58
  11.5 2.0 %collective-permute-done = f32[16,1,4096]{2,1,0:T(1,128)S(1)} collective-permute-done((f32[16,1,4096]{2,1,0:T(1,128)S(1)}, f32[16,1,4096]{2,1,0:T(1,128)S(1)}, u32[]{:S(2)}, u32[]{:S(2)}) %collective-permute-start) | collective-permute-done | bytes 262176 | tf_op jit(solution)/shard_map/ppermute | solution.py:20
  13.5 5.0 %collective-permute-done.1 = f32[16,1,4096]{2,1,0:T(1,128)} collective-permute-done((f32[16,1,4096]{2,1,0:T(1,128)S(1)}, f32[16,1,4096]{2,1,0:T(1,128)}, u32[]{:S(2)}, u32[]{:S(2)}) %collective-permute-start.1) | collective-permute-done | bytes 262176 | tf_op jit(solution)/shard_map/ppermute | solution.py:17
  18.5 2.4 %broadcast_multiply_fusion = (f32[16,2,4096]{2,1,0:T(2,128)S(1)}, f32[16,2,4096]{2,1,0:T(2,128)S(1)}) fusion(f32[16,2,4096]{2,1,0:T(2,128)S(1)} %copy-done, f32[2,4096]{1,0:T(2,128)S(1)} %copy-done.1, f32[16,2,4096]{2,1,0:T(2,128)S(1)} %add.58, f32[16,1,4096]{2,1,0:T(1,128)} %collective-permute-done.1, f32[16,1,4096]{2,1,0:T(1,128)S(1)} %collective-permute-done), kind=kLoop, calls=%fused_computation.26 | loop fusion | flops 1572864 | bytes 2654208 | tf_op jit(solution)/shard_map/div | solution.py:43
  21.0 0.6 reshape.36
  22.5 1.3 %fusion.23 = (f32[16,1,4096]{2,1,0:T(1,128)}, f32[16,1,4096]{2,1,0:T(1,128)}) fusion(f32[16,2,4096]{2,1,0:T(2,128)S(1)} %get-tuple-element.5), kind=kLoop, calls=%fused_computation.41 | loop fusion | bytes 1048576 | tf_op jit(solution)/shard_map/slice | solution.py:20
  23.9 3.5 %collective-permute-start.2 = (f32[16,1,4096]{2,1,0:T(1,128)}, f32[16,1,4096]{2,1,0:T(1,128)S(1)}, u32[]{:S(2)}, u32[]{:S(2)}) collective-permute-start(f32[16,1,4096]{2,1,0:T(1,128)} %get-tuple-element.23), channel_id=1, source_target_pairs={{1,0},{2,1},{3,2},{4,3},{5,4},{6,5},{7,6},{0,7},{9,8},{10,9},{11,1... | collective-permute-start | bytes 786440 | tf_op jit(solution)/shard_map/ppermute | solution.py:20
  27.4 0.9 fusion.6
  28.2 0.5 add.65
  28.8 8.5 %collective-permute-done.2 = f32[16,1,4096]{2,1,0:T(1,128)S(1)} collective-permute-done((f32[16,1,4096]{2,1,0:T(1,128)}, f32[16,1,4096]{2,1,0:T(1,128)S(1)}, u32[]{:S(2)}, u32[]{:S(2)}) %collective-permute-start.2) | collective-permute-done | bytes 262176 | tf_op jit(solution)/shard_map/ppermute | solution.py:20
  37.5 2.6 %subtract_convert_fusion = bf16[16,2,4096]{2,1,0:T(2,128)(2,1)S(1)} fusion(f32[16,2,4096]{2,1,0:T(2,128)S(1)} %copy-done, f32[16,2,4096]{2,1,0:T(2,128)S(1)} %get-tuple-element.6, f32[16,2,4096]{2,1,0:T(2,128)S(1)} %add.65, f32[16,2,4096]{2,1,0:T(2,128)S(1)} %get-tuple-element.5, f32[16,1,4096]{2,1,0:T(1,128)} %collective-permute-done.3, ...), kind=kLoop, calls=%fused_computation.24 | loop fusion | flops 1835008 | bytes 2916352 | tf_op jit(solution)/shard_map/convert_element_type | solution.py:49
  40.3 8.6 %all_to_all.35 = bf16[16,4,2048]{2,0,1:T(8,128)(2,1)S(1)} all-to-all(bf16[16,4,2048]{2,0,1:T(8,128)(2,1)S(1)} %copy.7), channel_id=1, replica_groups=mesh['band'=4,'grid'=8] {'band'}, dimensions={1} | all-to-all | bytes 524288 | tf_op jit(solution)/shard_map/all_to_all | solution.py:50
  49.1 39.0 %psum.7 = f32[64,64]{1,0:T(8,128)S(1)} all-reduce(f32[64,64]{1,0:T(8,128)S(1)} %convolution_multiply_fusion.2), channel_id=1, replica_groups=mesh['band'=4,'grid'=8] {'band','grid'}, use_global_device_ids=true, to_apply=%region_0.1 | all-reduce | flops 4096 | bytes 32768 | tf_op jit(solution)/shard_map/psum | solution.py:58
  88.2 0.6 reduce_max.9
  88.8 0.8 fusion.1
  89.6 0.8 fusion.14
  91.9 9.4 %all_to_all.36 = bf16[4,16,2048]{2,1,0:T(8,128)(2,1)S(1)} all-to-all(bf16[4,16,2048]{2,1,0:T(8,128)(2,1)S(1)} %bitcast.21), channel_id=1, replica_groups=mesh['band'=4,'grid'=8] {'band'}, dimensions={0} | all-to-all | bytes 524288 | tf_op jit(solution)/shard_map/all_to_all | solution.py:72
  101.5 0.9 reshape.37
  (23 shorter events, 3.3 us)
Async XLA Ops:
  0.0 7.9 %copy-start = (f32[16,2,4096]{2,1,0:T(2,128)S(1)}, f32[16,2,4096]{2,1,0:T(2,128)}, u32[]{:S(2)}) copy-start(f32[16,2,4096]{2,1,0:T(2,128)} %param.2) | copy-start | bytes 1572868
  1.9 11.6 %collective-permute-start = (f32[16,1,4096]{2,1,0:T(1,128)S(1)}, f32[16,1,4096]{2,1,0:T(1,128)S(1)}, u32[]{:S(2)}, u32[]{:S(2)}) collective-permute-start(f32[16,1,4096]{2,1,0:T(1,128)S(1)} %get-tuple-element.25), channel_id=1, source_target_pairs={{1,0},{2,1},{3,2},{4,3},{5,4},{6,5},{7,6},{0,7},{9,8},{10,9},{11,1... | collective-permute-start | bytes 786440 | tf_op jit(solution)/shard_map/ppermute | solution.py:20
  7.9 10.6 %collective-permute-start.1 = (f32[16,1,4096]{2,1,0:T(1,128)S(1)}, f32[16,1,4096]{2,1,0:T(1,128)}, u32[]{:S(2)}, u32[]{:S(2)}) collective-permute-start(f32[16,1,4096]{2,1,0:T(1,128)S(1)} %get-tuple-element.26), channel_id=1, source_target_pairs={{0,1},{1,2},{2,3},{3,4},{4,5},{5,6},{6,7},{7,0},{8,9},{9,10},{10,1... | collective-permute-start | bytes 786440 | tf_op jit(solution)/shard_map/ppermute | solution.py:17
  9.3 0.8 copy-start.1
  23.9 13.4 %collective-permute-start.2 = (f32[16,1,4096]{2,1,0:T(1,128)}, f32[16,1,4096]{2,1,0:T(1,128)S(1)}, u32[]{:S(2)}, u32[]{:S(2)}) collective-permute-start(f32[16,1,4096]{2,1,0:T(1,128)} %get-tuple-element.23), channel_id=1, source_target_pairs={{1,0},{2,1},{3,2},{4,3},{5,4},{6,5},{7,6},{0,7},{9,8},{10,9},{11,1... | collective-permute-start | bytes 786440 | tf_op jit(solution)/shard_map/ppermute | solution.py:20
  27.3 10.2 %collective-permute-start.3 = (f32[16,1,4096]{2,1,0:T(1,128)}, f32[16,1,4096]{2,1,0:T(1,128)}, u32[]{:S(2)}, u32[]{:S(2)}) collective-permute-start(f32[16,1,4096]{2,1,0:T(1,128)} %get-tuple-element.24), channel_id=1, source_target_pairs={{0,1},{1,2},{2,3},{3,4},{4,5},{5,6},{6,7},{7,0},{8,9},{9,10},{10,1... | collective-permute-start | bytes 786440 | tf_op jit(solution)/shard_map/ppermute | solution.py:17
where the time goes:
time: 103 us; the launch traced here: 102 us
  blocking collectives  56.9 us (55%)
  waiting for transfers between devices  15.7 us (15%)
  starting transfers between devices  9.52 us (9%)
  local copies, waits for them, and re-layouts  9.32 us (9%)
  other arithmetic  7.48 us (7%)
  matrix products  2.54 us (2%)
    psum x1, blocking collectives, local(): gram = lax.psum(partial_value, ('band', 'grid'))  39 us
    ppermute x2, waiting for transfers between devices, with_halo(): lax.ppermute(lax.slice_in_dim(block, 0, width, axis=dim), axis, backward)  10.5 us
    ppermute x2, starting transfers between devices, with_halo(): lax.ppermute(lax.slice_in_dim(block, 0, width, axis=dim), axis, backward)  9.51 us
    all_to_all x1, blocking collectives, local(): lax.all_to_all(turned, 'band', split_axis=0, concat_axis=1, tiled=True)  9.36 us
    all_to_all x1, blocking collectives, local(): lax.all_to_all(filtered, 'band', split_axis=1, concat_axis=0, tiled=True)  8.59 us
    ppermute x2, waiting for transfers between devices, with_halo(): lax.ppermute(lax.slice_in_dim(block, block.shape[dim] - width, None, axis...  5.27 us
    slice x2, local copies, waits for them, and re-layouts, with_halo(): lax.slice_in_dim(block, 0, width, axis=dim)  3.21 us
    convert_element_type x1, other arithmetic, local(): filtered = current.astype(jnp.bfloat16).reshape(count, zplanes * width)  2.58 us
  transfers between devices with their start and end apart: 4, of which 4 were waited for; matrix products, arithmetic and copies ran while one was open for 4% of the time, Pallas kernels for 0%

commit v1 on v0

--- a/solution.py
+++ b/solution.py
@@ -55,7 +55,7 @@
         )
         / total_cells
     )
-    gram = lax.psum(partial_value, ("band", "grid"))
+    gram = jnp.sum(lax.all_gather(partial_value, ("band", "grid")), axis=0)
     scale = jnp.max(jnp.sum(jnp.abs(gram), axis=1))
     identity_mat = jnp.eye(gram.shape[0], dtype=jnp.float32)
     upper = gram / scale

time: 103 us -> 135 us (1.31)
  blocking collectives: 56.9 us -> 89.2 us
    all_gather x0 -> x1, blocking collectives: none -> 72.2 us  [local(): gram = jnp.sum(lax.all_gather(partial_value, ('band', 'grid')), axis=0)]
    psum x1 -> x0, blocking collectives: 39 us -> none  [local(): gram = lax.psum(partial_value, ('band', 'grid'))]
  transfers between devices with their start and end apart: 4 -> 4, of which waited for: 4 -> 4; matrix products, arithmetic and copies ran while one was open for 4% -> 3% of each run, Pallas kernels for 0% -> 0%
where the time goes in v1:
time: 135 us
  blocking collectives  89.2 us (66%)
  waiting for transfers between devices  15.7 us (12%)
  starting transfers between devices  9.52 us (7%)
  local copies, waits for them, and re-layouts  9.32 us (7%)
  other arithmetic  7.57 us (6%)
  matrix products  2.54 us (2%)
    all_gather x1, blocking collectives, local(): gram = jnp.sum(lax.all_gather(partial_value, ('band', 'grid')), axis=0)  72.2 us
    ppermute x2, waiting for transfers between devices, with_halo(): lax.ppermute(lax.slice_in_dim(block, 0, width, axis=dim), axis, backward)  10.5 us
    ppermute x2, starting transfers between devices, with_halo(): lax.ppermute(lax.slice_in_dim(block, 0, width, axis=dim), axis, backward)  9.51 us
    all_to_all x1, blocking collectives, local(): lax.all_to_all(filtered, 'band', split_axis=1, concat_axis=0, tiled=True)  8.59 us
    all_to_all x1, blocking collectives, local(): lax.all_to_all(turned, 'band', split_axis=0, concat_axis=1, tiled=True)  8.39 us
    ppermute x2, waiting for transfers between devices, with_halo(): lax.ppermute(lax.slice_in_dim(block, block.shape[dim] - width, None, axis...  5.27 us
    slice x2, local copies, waits for them, and re-layouts, with_halo(): lax.slice_in_dim(block, 0, width, axis=dim)  3.21 us
  transfers between devices with their start and end apart: 4, of which 4 were waited for; matrix products, arithmetic and copies ran while one was open for 3% of the time, Pallas kernels for 0%

profile of v1, /device:TPU:0, one launch (start us, length us, event | category | flops | bytes accessed | tf_op | source)
XLA Modules:
  0.0 134.7 jit_solution(11696370182459699822)
XLA Ops:
  0.0 1.9 %fusion.24 = (f32[16,1,4096]{2,1,0:T(1,128)S(1)}, f32[16,1,4096]{2,1,0:T(1,128)S(1)}) fusion(f32[16,2,4096]{2,1,0:T(2,128)} %param.2), kind=kLoop, calls=%fused_computation.42 | loop fusion | bytes 1048576 | tf_op jit(solution)/shard_map/slice | solution.py:20
  1.9 6.1 %collective-permute-start = (f32[16,1,4096]{2,1,0:T(1,128)S(1)}, f32[16,1,4096]{2,1,0:T(1,128)S(1)}, u32[]{:S(2)}, u32[]{:S(2)}) collective-permute-start(f32[16,1,4096]{2,1,0:T(1,128)S(1)} %get-tuple-element.25), channel_id=1, source_target_pairs={{1,0},{2,1},{3,2},{4,3},{5,4},{6,5},{7,6},{0,7},{9,8},{10,9},{11,1... | collective-permute-start | bytes 786440 | tf_op jit(solution)/shard_map/ppermute | solution.py:20
  7.9 0.6 reshape.35
  8.6 0.4 fusion.19
  9.5 0.5 copy-done.1
  10.1 0.9 fusion.4
  11.0 0.5 add.56
  11.5 2.0 %collective-permute-done = f32[16,1,4096]{2,1,0:T(1,128)S(1)} collective-permute-done((f32[16,1,4096]{2,1,0:T(1,128)S(1)}, f32[16,1,4096]{2,1,0:T(1,128)S(1)}, u32[]{:S(2)}, u32[]{:S(2)}) %collective-permute-start) | collective-permute-done | bytes 262176 | tf_op jit(solution)/shard_map/ppermute | solution.py:20
  13.5 5.0 %collective-permute-done.1 = f32[16,1,4096]{2,1,0:T(1,128)} collective-permute-done((f32[16,1,4096]{2,1,0:T(1,128)S(1)}, f32[16,1,4096]{2,1,0:T(1,128)}, u32[]{:S(2)}, u32[]{:S(2)}) %collective-permute-start.1) | collective-permute-done | bytes 262176 | tf_op jit(solution)/shard_map/ppermute | solution.py:17
  18.5 2.4 %broadcast_multiply_fusion = (f32[16,2,4096]{2,1,0:T(2,128)S(1)}, f32[16,2,4096]{2,1,0:T(2,128)S(1)}) fusion(f32[16,2,4096]{2,1,0:T(2,128)S(1)} %copy-done, f32[2,4096]{1,0:T(2,128)S(1)} %copy-done.1, f32[16,2,4096]{2,1,0:T(2,128)S(1)} %add.56, f32[16,1,4096]{2,1,0:T(1,128)} %collective-permute-done.1, f32[16,1,4096]{2,1,0:T(1,128)S(1)} %collective-permute-done), kind=kLoop, calls=%fused_computation.26 | loop fusion | flops 1572864 | bytes 2654208 | tf_op jit(solution)/shard_map/div | solution.py:43
  21.0 0.6 reshape.36
  22.5 1.3 fusion.23
  23.9 3.5 %collective-permute-start.2 = (f32[16,1,4096]{2,1,0:T(1,128)}, f32[16,1,4096]{2,1,0:T(1,128)S(1)}, u32[]{:S(2)}, u32[]{:S(2)}) collective-permute-start(f32[16,1,4096]{2,1,0:T(1,128)} %get-tuple-element.23), channel_id=1, source_target_pairs={{1,0},{2,1},{3,2},{4,3},{5,4},{6,5},{7,6},{0,7},{9,8},{10,9},{11,1... | collective-permute-start | bytes 786440 | tf_op jit(solution)/shard_map/ppermute | solution.py:20
  27.4 0.9 fusion.6
  28.2 0.5 add.63
  28.8 8.5 %collective-permute-done.2 = f32[16,1,4096]{2,1,0:T(1,128)S(1)} collective-permute-done((f32[16,1,4096]{2,1,0:T(1,128)}, f32[16,1,4096]{2,1,0:T(1,128)S(1)}, u32[]{:S(2)}, u32[]{:S(2)}) %collective-permute-start.2) | collective-permute-done | bytes 262176 | tf_op jit(solution)/shard_map/ppermute | solution.py:20
  37.5 2.6 %subtract_convert_fusion = bf16[16,2,4096]{2,1,0:T(2,128)(2,1)S(1)} fusion(f32[16,2,4096]{2,1,0:T(2,128)S(1)} %copy-done, f32[16,2,4096]{2,1,0:T(2,128)S(1)} %get-tuple-element.6, f32[16,2,4096]{2,1,0:T(2,128)S(1)} %add.63, f32[16,2,4096]{2,1,0:T(2,128)S(1)} %get-tuple-element.5, f32[16,1,4096]{2,1,0:T(1,128)} %collective-permute-done.3, ...), kind=kLoop, calls=%fused_computation.24 | loop fusion | flops 1835008 | bytes 2916352 | tf_op jit(solution)/shard_map/convert_element_type | solution.py:49
  40.3 8.6 %all_to_all.35 = bf16[16,4,2048]{2,0,1:T(8,128)(2,1)S(1)} all-to-all(bf16[16,4,2048]{2,0,1:T(8,128)(2,1)S(1)} %copy.9), channel_id=1, replica_groups=mesh['band'=4,'grid'=8] {'band'}, dimensions={1} | all-to-all | bytes 524288 | tf_op jit(solution)/shard_map/all_to_all | solution.py:50
  49.1 72.2 %all-gather = f32[2048,64]{1,0:T(8,128)S(1)} all-gather(f32[64,64]{1,0:T(8,128)S(1)} %convolution_multiply_fusion.2), channel_id=2, replica_groups=mesh['band'=4,'grid'=8] {'band','grid'}, dimensions={0}, use_global_device_ids=true | all-gather | bytes 540672 | tf_op jit(solution)/shard_map/all_gather | solution.py:58
  121.5 0.6 reduce_max.9
  122.2 0.8 fusion.1
  123.0 0.8 fusion.14
  125.2 8.4 %all_to_all.36 = bf16[4,16,2048]{2,1,0:T(8,128)(2,1)S(1)} all-to-all(bf16[4,16,2048]{2,1,0:T(8,128)(2,1)S(1)} %bitcast.23), channel_id=1, replica_groups=mesh['band'=4,'grid'=8] {'band'}, dimensions={0} | all-to-all | bytes 524288 | tf_op jit(solution)/shard_map/all_to_all | solution.py:72
  133.8 0.9 reshape.37
  (24 shorter events, 3.4 us)
Async XLA Ops:
  0.0 7.9 %copy-start = (f32[16,2,4096]{2,1,0:T(2,128)S(1)}, f32[16,2,4096]{2,1,0:T(2,128)}, u32[]{:S(2)}) copy-start(f32[16,2,4096]{2,1,0:T(2,128)} %param.2) | copy-start | bytes 1572868
  1.9 11.6 %collective-permute-start = (f32[16,1,4096]{2,1,0:T(1,128)S(1)}, f32[16,1,4096]{2,1,0:T(1,128)S(1)}, u32[]{:S(2)}, u32[]{:S(2)}) collective-permute-start(f32[16,1,4096]{2,1,0:T(1,128)S(1)} %get-tuple-element.25), channel_id=1, source_target_pairs={{1,0},{2,1},{3,2},{4,3},{5,4},{6,5},{7,6},{0,7},{9,8},{10,9},{11,1... | collective-permute-start | bytes 786440 | tf_op jit(solution)/shard_map/ppermute | solution.py:20
  7.9 10.6 %collective-permute-start.1 = (f32[16,1,4096]{2,1,0:T(1,128)S(1)}, f32[16,1,4096]{2,1,0:T(1,128)}, u32[]{:S(2)}, u32[]{:S(2)}) collective-permute-start(f32[16,1,4096]{2,1,0:T(1,128)S(1)} %get-tuple-element.26), channel_id=1, source_target_pairs={{0,1},{1,2},{2,3},{3,4},{4,5},{5,6},{6,7},{7,0},{8,9},{9,10},{10,1... | collective-permute-start | bytes 786440 | tf_op jit(solution)/shard_map/ppermute | solution.py:17
  9.3 0.8 copy-start.1
  23.9 13.4 %collective-permute-start.2 = (f32[16,1,4096]{2,1,0:T(1,128)}, f32[16,1,4096]{2,1,0:T(1,128)S(1)}, u32[]{:S(2)}, u32[]{:S(2)}) collective-permute-start(f32[16,1,4096]{2,1,0:T(1,128)} %get-tuple-element.23), channel_id=1, source_target_pairs={{1,0},{2,1},{3,2},{4,3},{5,4},{6,5},{7,6},{0,7},{9,8},{10,9},{11,1... | collective-permute-start | bytes 786440 | tf_op jit(solution)/shard_map/ppermute | solution.py:20
  27.3 10.2 %collective-permute-start.3 = (f32[16,1,4096]{2,1,0:T(1,128)}, f32[16,1,4096]{2,1,0:T(1,128)}, u32[]{:S(2)}, u32[]{:S(2)}) collective-permute-start(f32[16,1,4096]{2,1,0:T(1,128)} %get-tuple-element.24), channel_id=1, source_target_pairs={{0,1},{1,2},{2,3},{3,4},{4,5},{5,6},{6,7},{7,0},{8,9},{9,10},{10,1... | collective-permute-start | bytes 786440 | tf_op jit(solution)/shard_map/ppermute | solution.py:17
